TPU v7x, 256 devices: a whole 4x4x8 slice. The times are simulated.
256 devices in a mesh: train: 16 (over z, core), query: 16 (over y, x).
Axes of the slice: x: 4, y: 4, z: 8, core: 2. Of those that a mesh axis runs over, the one named last changes fastest.
Arguments:
- train_hidden: bfloat16 [512, 96, 4096], P(('train', 'query')), may hold values from -6 to 6
- train_outgrad: bfloat16 [512, 96, 14336], P(('train', 'query')), may hold values from -6 to 6
- train_mask: int32 [512, 96], P(('train', 'query')), may hold values 0 or 1
- query_hidden: bfloat16 [256, 96, 4096], P(('train', 'query')), may hold values from -6 to 6
- query_outgrad: bfloat16 [256, 96, 14336], P(('train', 'query')), may hold values from -6 to 6
- query_mask: int32 [256, 96], P(('train', 'query')), may hold values 0 or 1
- proj_in: bfloat16 [4096, 64], replicated, may hold values from -0.09375 to 0.09375
- proj_out: bfloat16 [14336, 64], replicated, may hold values from -0.046875 to 0.046875
Outputs:
- scores: float32 [512, 256], P(('train', 'query'))
All inputs are finite; a program needn't handle non-finite values. No bound on the sum of `train_mask` or of `query_mask` on one device may be relied on, other than what follows from the above.
Results may differ from a plain program's by a relative error of at most 0.0003.
Values sent between devices are 32-bit elements; how exact they have to be, the bound alone decides.
A program may use at most 128 MiB of HBM per device.

v0:
```python
import jax
import jax.numpy as jnp
from jax import lax
from jax.sharding import PartitionSpec as P

damping_share = 0.1


def sketch_terms(hidden, outgrad, mask, proj_in, proj_out):
    proof_count, token_count, model_width = hidden.shape
    input_side = jnp.dot(
        hidden.reshape(proof_count * token_count, model_width),
        proj_in,
        preferred_element_type=jnp.float32,
    )
    output_side = jnp.dot(
        outgrad.reshape(proof_count * token_count, -1), proj_out, preferred_element_type=jnp.float32
    )
    output_side = output_side * mask.reshape(-1, 1).astype(jnp.float32)
    input_side = input_side.reshape(proof_count, token_count, -1)
    output_side = output_side.reshape(proof_count, token_count, -1)
    outer_sum = jnp.einsum("pti,ptj->pij", output_side, input_side, precision=lax.Precision.HIGHEST)
    return outer_sum.reshape(proof_count, -1)


def chol_solve(factor, right):
    lower_solved = lax.linalg.triangular_solve(factor, right, left_side=True, lower=True)
    return lax.linalg.triangular_solve(
        factor, lower_solved, left_side=True, lower=True, transpose_a=True
    )


def body(
    train_hidden,
    train_outgrad,
    train_mask,
    query_hidden,
    query_outgrad,
    query_mask,
    proj_in,
    proj_out,
):
    train_sketch = sketch_terms(train_hidden, train_outgrad, train_mask, proj_in, proj_out)
    query_sketch = sketch_terms(query_hidden, query_outgrad, query_mask, proj_in, proj_out)
    block_rows = train_sketch.shape[0]
    everyone, all_queries = (
        lax.all_gather(train_sketch, ("train", "query"), axis=0, tiled=True),
        lax.all_gather(query_sketch, ("train", "query"), axis=0, tiled=True),
    )
    gram_matrix = jnp.dot(everyone, everyone.T, precision=lax.Precision.HIGHEST)
    products = jnp.dot(everyone, all_queries.T, precision=lax.Precision.HIGHEST)
    total_rows = gram_matrix.shape[0]
    damping = damping_share * jnp.trace(gram_matrix) / total_rows
    system = gram_matrix + damping * jnp.eye(total_rows, dtype=jnp.float32)
    factor = jnp.linalg.cholesky(system)
    solved = total_rows * chol_solve(factor, products)
    return lax.dynamic_slice_in_dim(
        solved, lax.axis_index(("train", "query")) * block_rows, block_rows, 0
    )


def solution(mesh):
    in_specs = (
        P(("train", "query"), None, None),
        P(("train", "query"), None, None),
        P(("train", "query"), None),
        P(("train", "query"), None, None),
        P(("train", "query"), None, None),
        P(("train", "query"), None),
        P(),
        P(),
    )
    out_specs = P(("train", "query"), None)
    return jax.shard_map(body, mesh=mesh, in_specs=in_specs, out_specs=out_specs, check_vma=False)
```

profile of v0, /device:TPU:1, one launch (start us, length us, event | category | flops | bytes accessed | tf_op | source)
XLA Modules:
  0.0 341.7 jit_solution(4151892252313201515)
XLA Ops:
  6.5 0.8 convert_element_type.23
  7.4 0.1 convert_element_type.24
  7.5 5.1 %convolution_multiply_fusion = f32[192,64]{0,1:T(8,128)S(1)} fusion(bf16[192,14336]{1,0:T(8,128)(2,1)} %bitcast.89, bf16[14336,64]{0,1:T(8,128)(2,1)} %param.15, f32[192]{0:T(256)S(1)} %convert_element_type.24), kind=kOutput, calls=%fused_computation.18 | convolution fusion | flops 352333824 | bytes 7389952 | tf_op jit(solution)/shard_map/dot_general | solution.py:16
  12.5 0.1 reshape.92
  12.6 2.1 fusion.12
  14.7 0.2 fusion.49
  15.0 0.7 reshape.116
  15.8 1.5 fusion.10
  17.3 2.4 fusion.5
  19.6 0.2 fusion.67
  19.9 0.7 reshape.118
  20.6 117.2 %all-gather.5.cloned.1.call-done = f32[256,2,4096]{2,1,0:T(2,128)} async-done(((f32[1,2,4096]{2,1,0:T(2,128)}), f32[256,2,4096]{2,1,0:T(2,128)}) %all-gather.5.cloned.1.call-update) | async-done | bytes 8388624 | tf_op jit(solution)/shard_map/all_gather | solution.py:47
  137.9 10.9 %reshape.117 = f32[512,4096]{1,0:T(8,128)} reshape(f32[256,2,4096]{2,1,0:T(2,128)} %all-gather.5.cloned.1.call-done) | data formatting | bytes 16777216
  148.7 18.6 %select_reduce_fusion = (f32[]{:T(128)}, f32[512,512]{1,0:T(8,128)}) fusion(f32[512,4096]{1,0:T(8,128)} %reshape.117), kind=kOutput, calls=%fused_computation.25 | convolution fusion | flops 12885688320 | bytes 9437188 | tf_op jit(solution)/shard_map/dot_general | solution.py:50
  167.3 2.5 copy.12
  170.5 1.8 fusion.9
  172.3 1.1 copy-done.2
  173.4 11.7 %cholesky.103 = f32[128,128]{1,0:T(8,128)S(1)} custom-call(f32[128,128]{1,0:T(8,128)S(1)} %cholesky.263), custom_call_target="Cholesky" | custom-call | tf_op jit(solution)/shard_map/jit(cholesky)/cholesky | solution.py:55
  185.1 9.8 %custom-call.32 = f32[1,128,128]{1,2,0:T(8,128)S(1)} custom-call(f32[1,128,128]{2,1,0:T(8,128)S(1)} %get-tuple-element.32), custom_call_target="InvertDiagBlocksLowerTriangular" | custom-call | tf_op jit(solution)/shard_map/jit(cholesky)/cholesky | solution.py:55
  195.0 1.1 cholesky.222
  196.1 1.9 constant_dynamic-update-slice_fusion
  198.0 1.3 convolution_subtract_fusion
  199.3 11.7 %cholesky.215 = f32[128,128]{1,0:T(8,128)S(1)} custom-call(f32[128,128]{1,0:T(8,128)S(1)} %cholesky.267), custom_call_target="Cholesky" | custom-call | tf_op jit(solution)/shard_map/jit(cholesky)/cholesky | solution.py:55
  211.0 0.6 select_reduce_fusion.3
  211.6 9.9 %custom-call.33 = f32[1,128,128]{1,2,0:T(8,128)S(1)} custom-call(f32[1,128,128]{2,1,0:T(8,128)S(1)} %get-tuple-element.29), custom_call_target="InvertDiagBlocksLowerTriangular" | custom-call | tf_op jit(solution)/shard_map/jit(cholesky)/cholesky | solution.py:55
  221.6 1.0 convolution_dynamic-update-slice_fusion
  222.6 1.4 convolution_subtract_fusion.5
  224.0 11.7 %cholesky.236 = f32[128,128]{1,0:T(8,128)S(1)} custom-call(f32[128,128]{1,0:T(8,128)S(1)} %cholesky.272), custom_call_target="Cholesky" | custom-call | tf_op jit(solution)/shard_map/jit(cholesky)/cholesky | solution.py:55
  235.7 0.6 select_reduce_fusion.2
  236.4 9.8 %custom-call.34 = f32[1,128,128]{1,2,0:T(8,128)S(1)} custom-call(f32[1,128,128]{2,1,0:T(8,128)S(1)} %get-tuple-element.26), custom_call_target="InvertDiagBlocksLowerTriangular" | custom-call | tf_op jit(solution)/shard_map/jit(cholesky)/cholesky | solution.py:55
  246.2 0.9 convolution_dynamic-update-slice_fusion.1
  247.0 1.4 convolution_subtract_fusion.8
  248.4 11.7 %cholesky.253 = f32[128,128]{1,0:T(8,128)S(1)} custom-call(f32[128,128]{1,0:T(8,128)S(1)} %convolution_subtract_fusion.8), custom_call_target="Cholesky" | custom-call | tf_op jit(solution)/shard_map/jit(cholesky)/cholesky | solution.py:55
  260.1 0.7 compare_reduce_fusion.2
  262.0 0.6 compare_reduce_fusion.1
  263.2 0.6 select_reduce_fusion.1
  263.8 0.6 compare_reduce_fusion
  265.0 2.6 select_select_fusion
  267.6 11.9 %while.1 = (s32[]{:T(128)}, f32[512,512]{1,0:T(8,128)}, s32[4,2]{0,1:T(2,128)S(1)}, f32[4,128,128]{2,1,0:T(8,128)S(1)}, s32[]{:T(128)}) while((s32[]{:T(128)}, f32[512,512]{1,0:T(8,128)}, s32[4,2]{0,1:T(2,128)S(1)}, f32[4,128,128]{2,1,0:T(8,128)S(1)}, s32[]{:T(128)}) %tuple.28), condition=%wide.while_cond, body=%wide.while_body.sunk | while | flops 2 | bytes 131181 | solution.py:28
  267.7 0.6 fusion.90
  268.3 2.3 bitcast_dynamic-update-slice_fusion.2
  270.7 0.6 fusion.90
  271.3 2.3 bitcast_dynamic-update-slice_fusion.2
  273.7 0.6 fusion.90
  274.3 2.3 bitcast_dynamic-update-slice_fusion.2
  276.7 0.6 fusion.90
  277.3 2.2 bitcast_dynamic-update-slice_fusion.2
  279.5 39.3 %custom-call.35 = f32[4,128,128]{1,2,0:T(8,128)S(1)} custom-call(f32[4,128,128]{2,1,0:T(8,128)S(1)} %get-tuple-element.12), custom_call_target="InvertDiagBlocksLowerTriangular" | custom-call | tf_op jit(solution)/shard_map/triangular_solve | solution.py:28
  318.9 10.6 %fusion = f32[512,256]{1,0:T(8,128)S(1)} fusion(f32[512,4096]{1,0:T(8,128)} %reshape.117, f32[256,1,4096]{2,1,0:T(1,128)} %all-gather.7.cloned.1.call-done), kind=kOutput, calls=%fused_computation.2 | convolution fusion | flops 6442450944 | bytes 13107200 | tf_op jit(solution)/shard_map/dot_general | solution.py:51
  329.4 0.3 fusion.38
  329.8 0.3 convolution_subtract_fusion.7
  330.0 0.3 fusion.53
  330.3 0.3 convolution_subtract_fusion.4
  330.6 0.3 fusion.55
  331.0 0.4 convolution_subtract_fusion.3
  331.4 0.3 fusion.57
  331.7 0.3 fusion.56
  331.9 0.3 convolution_subtract_fusion.6
  332.3 0.3 fusion.54
  332.5 0.4 convolution_subtract_fusion.2
  332.9 0.3 fusion.52
  333.2 0.5 convolution_subtract_fusion.1
  333.7 0.3 fusion.51
  334.0 0.6 fusion.61
  (26 shorter events, 0.5 us)
Async XLA Ops:
  6.5 10.7 %copy-start = (bf16[1,96,14336]{2,1,0:T(8,128)(2,1)S(1)}, bf16[1,96,14336]{2,1,0:T(8,128)(2,1)}, u32[]{:S(2)}) copy-start(bf16[1,96,14336]{2,1,0:T(8,128)(2,1)} %param.12) | copy-start | bytes 8257540
  6.5 131.3 %all-gather.5.cloned.1.call-start = ((), (), s32[]{:S(2)}) async-start(), calls=%async_computation | async-start | bytes 8421376 | tf_op jit(solution)/shard_map/all_gather | solution.py:47
  7.5 5.2 %copy-start.3 = (bf16[4096,64]{0,1:T(8,128)(2,1)S(1)}, bf16[4096,64]{0,1:T(8,128)(2,1)}, u32[]{:S(2)}) copy-start(bf16[4096,64]{0,1:T(8,128)(2,1)} %param.14) | copy-start | bytes 1572868
  7.5 8.3 %copy-start.4 = (s32[1,96]{1,0:T(1,128)S(1)}, s32[1,96]{1,0:T(1,128)}, u32[]{:S(2)}) copy-start(s32[1,96]{1,0:T(1,128)} %param.13) | copy-start | bytes 1156
  15.7 303.2 %all-gather.7.cloned.1.call-start = ((), (), s32[]{:S(2)}) async-start(), calls=%async_computation.1 | async-start | bytes 4210688 | tf_op jit(solution)/shard_map/all_gather | solution.py:48
  172.3 1.1 copy-start.2
  318.9 10.9 %copy-start.1 = (f32[512,512]{1,0:T(8,128)S(1)}, f32[512,512]{1,0:T(8,128)}, u32[]{:S(2)}) copy-start(f32[512,512]{1,0:T(8,128)} %get-tuple-element.86) | copy-start | bytes 3145732
Sparse Core Ops, SparseCore 0:
  15.8 121.9 all-gather.4
  141.6 113.3 all-gather.6
where the time goes:
time: 348 us; the launch traced here: 342 us
  other arithmetic  125 us (36%)
  waiting for transfers between devices  117 us (34%)
  matrix products  52.9 us (15%)
  local copies, waits for them, and re-layouts  29 us (8%)
  between operations  17 us (5%)
    all_gather x1, waiting for transfers between devices, body(): lax.all_gather(train_sketch, ('train', 'query'), axis=0, tiled=True)  117 us
    another operation x14, other arithmetic, body(): factor = jnp.linalg.cholesky(system)  80.3 us
    another operation x3, other arithmetic, chol_solve(): lax.linalg.triangular_solve(factor, lower_solved, left_side=True, lower=T...  41.9 us
    dot_general x1, matrix products, body(): gram_matrix = jnp.dot(everyone, everyone.T, precision=lax.Precision.HIGHEST)  18.6 us
    unnamed x13, local copies, waits for them, and re-layouts  13.3 us
    another operation x12, local copies, waits for them, and re-layouts  11.8 us
    dot_general x1, matrix products, body(): products = jnp.dot(everyone, all_queries.T, precision=lax.Precision.HIGHEST)  10.6 us
    another operation x6, matrix products, body(): factor = jnp.linalg.cholesky(system)  7.84 us
  transfers between devices with their start and end apart: 2, of which 1 were waited for; matrix products, arithmetic and copies ran while one was open for 53% of the time, Pallas kernels for 0%

commit v1 on v0

--- a/solution.py
+++ b/solution.py
@@ -4,6 +4,7 @@
 from jax.sharding import PartitionSpec as P
 
 damping_share = 0.1
+AXES = ("train", "query")
 
 
 def sketch_terms(hidden, outgrad, mask, proj_in, proj_out):
@@ -43,32 +44,40 @@
     train_sketch = sketch_terms(train_hidden, train_outgrad, train_mask, proj_in, proj_out)
     query_sketch = sketch_terms(query_hidden, query_outgrad, query_mask, proj_in, proj_out)
     block_rows = train_sketch.shape[0]
-    everyone, all_queries = (
-        lax.all_gather(train_sketch, ("train", "query"), axis=0, tiled=True),
-        lax.all_gather(query_sketch, ("train", "query"), axis=0, tiled=True),
-    )
-    gram_matrix = jnp.dot(everyone, everyone.T, precision=lax.Precision.HIGHEST)
-    products = jnp.dot(everyone, all_queries.T, precision=lax.Precision.HIGHEST)
-    total_rows = gram_matrix.shape[0]
+    query_rows = query_sketch.shape[0]
+    devices = lax.axis_size(AXES)
+    width = train_sketch.shape[1]
+    chunk = width // devices
+    rows = jnp.concatenate([train_sketch, query_sketch], axis=0)
+    pieces = rows.reshape(block_rows + query_rows, devices, chunk).transpose(1, 0, 2)
+    gathered = lax.all_to_all(pieces, AXES, 0, 0, tiled=True)
+    train_cols = gathered[:, :block_rows, :].reshape(devices * block_rows, chunk)
+    query_cols = gathered[:, block_rows:, :].reshape(devices * query_rows, chunk)
+    both_cols = jnp.concatenate([train_cols, query_cols], axis=0)
+    partial = jnp.dot(train_cols, both_cols.T, precision=lax.Precision.HIGHEST)
+    summed = lax.psum(partial, AXES)
+    total_rows = devices * block_rows
+    gram_matrix = summed[:, :total_rows]
+    products = summed[:, total_rows:]
     damping = damping_share * jnp.trace(gram_matrix) / total_rows
     system = gram_matrix + damping * jnp.eye(total_rows, dtype=jnp.float32)
     factor = jnp.linalg.cholesky(system)
     solved = total_rows * chol_solve(factor, products)
     return lax.dynamic_slice_in_dim(
-        solved, lax.axis_index(("train", "query")) * block_rows, block_rows, 0
+        solved, lax.axis_index(AXES) * block_rows, block_rows, 0
     )
 
 
 def solution(mesh):
     in_specs = (
-        P(("train", "query"), None, None),
-        P(("train", "query"), None, None),
-        P(("train", "query"), None),
-        P(("train", "query"), None, None),
-        P(("train", "query"), None, None),
-        P(("train", "query"), None),
+        P(AXES, None, None),
+        P(AXES, None, None),
+        P(AXES, None),
+        P(AXES, None, None),
+        P(AXES, None, None),
+        P(AXES, None),
         P(),
         P(),
     )
-    out_specs = P(("train", "query"), None)
+    out_specs = P(AXES, None)
     return jax.shard_map(body, mesh=mesh, in_specs=in_specs, out_specs=out_specs, check_vma=False)

time: 348 us -> 493 us (1.42)
  waiting for transfers between devices: 117 us -> 254 us
  blocking collectives: 0 us -> 36.3 us
  matrix products: 52.9 us -> 30 us
  local copies, waits for them, and re-layouts: 29 us -> 22 us
    psum x0 -> x1, waiting for transfers between devices: none -> 254 us  [body(): summed = lax.psum(partial, AXES)]
    all_gather x2 -> x0, waiting for transfers between devices: 117 us -> none  [the longest x1 117 us: body(): lax.all_gather(train_sketch, ('train', 'query'), axis=0, tiled=True)]
    all_to_all x0 -> x1, blocking collectives: none -> 36.3 us  [body(): gathered = lax.all_to_all(pieces, AXES, 0, 0, tiled=True)]
    dot_general x2 -> x1, matrix products: 29.2 us -> 2.58 us  [body(): partial = jnp.dot(train_cols, both_cols.T, precision=lax.Precision.HIGHEST)]
    unnamed x13 -> x12, local copies, waits for them, and re-layouts: 13.3 us -> 1.96 us
    another operation x12 -> x20, local copies, waits for them, and re-layouts: 11.8 us -> 14.4 us
  transfers between devices with their start and end apart: 2 -> 1, of which waited for: 1 -> 1; matrix products, arithmetic and copies ran while one was open for 53% -> 0% of each run, Pallas kernels for 0% -> 0%
where the time goes in v1:
time: 493 us; the launch traced here: 488 us
  waiting for transfers between devices  254 us (52%)
  other arithmetic  129 us (26%)
  blocking collectives  36.3 us (7%)
  matrix products  30 us (6%)
  local copies, waits for them, and re-layouts  22 us (4%)
  between operations  17.2 us (3%)
    psum x1, waiting for transfers between devices, body(): summed = lax.psum(partial, AXES)  254 us
    another operation x14, other arithmetic, body(): factor = jnp.linalg.cholesky(system)  78.8 us
    another operation x3, other arithmetic, chol_solve(): lax.linalg.triangular_solve(factor, lower_solved, left_side=True, lower=T...  42.5 us
    all_to_all x1, blocking collectives, body(): gathered = lax.all_to_all(pieces, AXES, 0, 0, tiled=True)  36.3 us
    another operation x20, local copies, waits for them, and re-layouts  14.4 us
  transfers between devices with their start and end apart: 1, of which 1 were waited for; matrix products, arithmetic and copies ran while one was open for 0% of the time, Pallas kernels for 0%

profile of v1, /device:TPU:1, one launch (start us, length us, event | category | flops | bytes accessed | tf_op | source)
XLA Modules:
  0.0 487.8 jit_solution(16758990475845995787)
XLA Ops:
  6.5 0.8 convert_bitcast_fusion
  7.3 1.7 fusion.6
  9.1 2.7 fusion.2
  12.1 2.1 fusion.8
  14.3 5.0 %convolution_multiply_fusion = f32[192,64]{0,1:T(8,128)S(1)} fusion(bf16[192,14336]{1,0:T(8,128)(2,1)} %bitcast.84, bf16[14336,64]{0,1:T(8,128)(2,1)} %param.15, f32[192]{0:T(256)S(1)} %convert_element_type.24), kind=kOutput, calls=%fused_computation.15 | convolution fusion | flops 352333824 | bytes 7389952 | tf_op jit(solution)/shard_map/dot_general | solution.py:17
  19.4 0.2 fusion.45
  19.8 0.3 copy.52
  20.1 36.3 %all_to_all.5 = f32[256,3,16]{2,1,0:T(4,128)S(1)} all-to-all(f32[256,3,16]{2,1,0:T(4,128)S(1)} %copy.52), channel_id=1, replica_groups=mesh['train'=16,'query'=16] {'train','query'}, dimensions={0} | all-to-all | bytes 98304 | tf_op jit(solution)/shard_map/all_to_all | solution.py:53
  56.7 2.6 fusion.54
  59.4 253.5 %all-reduce.3.cloned.1.call-done = f32[512,768]{0,1:T(8,128)} async-done(((f32[512,768]{0,1:T(8,128)}), f32[512,768]{0,1:T(8,128)}) %all-reduce.3.cloned.1.call-update) | async-done | bytes 1572880 | tf_op jit(solution)/shard_map/psum | solution.py:58
  312.9 1.9 select_reduce_fusion
  315.4 2.3 select_add_fusion
  317.7 2.6 copy.56
  320.3 1.8 fusion.5
  322.1 1.0 copy-done.3
  323.0 11.7 %cholesky.103 = f32[128,128]{1,0:T(8,128)S(1)} custom-call(f32[128,128]{1,0:T(8,128)S(1)} %cholesky.263), custom_call_target="Cholesky" | custom-call | tf_op jit(solution)/shard_map/jit(cholesky)/cholesky | solution.py:64
  334.9 9.8 %custom-call.32 = f32[1,128,128]{1,2,0:T(8,128)S(1)} custom-call(f32[1,128,128]{2,1,0:T(8,128)S(1)} %get-tuple-element.44), custom_call_target="InvertDiagBlocksLowerTriangular" | custom-call | tf_op jit(solution)/shard_map/jit(cholesky)/cholesky | solution.py:64
  344.7 1.2 fusion.30
  346.1 1.3 convolution_subtract_fusion
  347.3 11.9 %cholesky.215 = f32[128,128]{1,0:T(8,128)S(1)} custom-call(f32[128,128]{1,0:T(8,128)S(1)} %cholesky.267), custom_call_target="Cholesky" | custom-call | tf_op jit(solution)/shard_map/jit(cholesky)/cholesky | solution.py:64
  359.3 9.8 %custom-call.33 = f32[1,128,128]{1,2,0:T(8,128)S(1)} custom-call(f32[1,128,128]{2,1,0:T(8,128)S(1)} %get-tuple-element.42), custom_call_target="InvertDiagBlocksLowerTriangular" | custom-call | tf_op jit(solution)/shard_map/jit(cholesky)/cholesky | solution.py:64
  369.3 0.3 convolution_dynamic-update-slice_fusion
  369.7 1.0 copy-done.1
  370.6 1.5 convolution_subtract_fusion.5
  372.2 11.7 %cholesky.236 = f32[128,128]{1,0:T(8,128)S(1)} custom-call(f32[128,128]{1,0:T(8,128)S(1)} %cholesky.272), custom_call_target="Cholesky" | custom-call | tf_op jit(solution)/shard_map/jit(cholesky)/cholesky | solution.py:64
  384.0 0.7 constant_dynamic-update-slice_fusion.1
  384.7 9.8 %custom-call.34 = f32[1,128,128]{1,2,0:T(8,128)S(1)} custom-call(f32[1,128,128]{2,1,0:T(8,128)S(1)} %get-tuple-element.40), custom_call_target="InvertDiagBlocksLowerTriangular" | custom-call | tf_op jit(solution)/shard_map/jit(cholesky)/cholesky | solution.py:64
  394.5 0.9 convolution_dynamic-update-slice_fusion.1
  395.4 1.5 convolution_subtract_fusion.8
  396.9 11.9 %cholesky.253 = f32[128,128]{1,0:T(8,128)S(1)} custom-call(f32[128,128]{1,0:T(8,128)S(1)} %convolution_subtract_fusion.8), custom_call_target="Cholesky" | custom-call | tf_op jit(solution)/shard_map/jit(cholesky)/cholesky | solution.py:64
  409.0 0.7 constant_dynamic-update-slice_fusion.2
  409.6 0.7 compare_reduce_fusion.1
  410.3 0.7 compare_reduce_fusion
  411.0 0.7 compare_reduce_fusion.2
  414.2 2.3 select_select_fusion
  416.5 14.5 %while.1 = (s32[]{:T(128)}, f32[512,512]{0,1:T(8,128)}, s32[4,2]{0,1:T(2,128)S(1)}, f32[4,128,128]{2,1,0:T(8,128)}, s32[]{:T(128)}) while((s32[]{:T(128)}, f32[512,512]{0,1:T(8,128)}, s32[4,2]{0,1:T(2,128)S(1)}, f32[4,128,128]{2,1,0:T(8,128)}, s32[]{:T(128)}) %tuple.27), condition=%wide.while_cond, body=%wide.while_body.sunk | while | flops 2 | bytes 393329 | solution.py:29
  416.6 0.6 fusion.89
  417.2 2.2 dynamic-slice.7
  419.5 0.6 bitcast_dynamic-update-slice_fusion.2
  420.2 0.6 fusion.89
  420.8 2.2 dynamic-slice.7
  423.2 0.6 bitcast_dynamic-update-slice_fusion.2
  423.9 0.6 fusion.89
  424.4 2.2 dynamic-slice.7
  426.8 0.6 bitcast_dynamic-update-slice_fusion.2
  427.5 0.6 fusion.89
  428.1 2.2 dynamic-slice.7
  430.4 0.6 bitcast_dynamic-update-slice_fusion.2
  431.0 40.1 %custom-call.35 = f32[4,128,128]{1,2,0:T(8,128)S(1)} custom-call(f32[4,128,128]{2,1,0:T(8,128)} %get-tuple-element.12), custom_call_target="InvertDiagBlocksLowerTriangular" | custom-call | tf_op jit(solution)/shard_map/triangular_solve | solution.py:29
  471.1 1.3 fusion.34
  472.4 1.3 convolution_subtract_fusion.7
  473.8 0.3 fusion.49
  474.1 1.6 convolution_subtract_fusion.4
  475.7 0.3 fusion.51
  476.0 1.7 convolution_subtract_fusion.3
  477.7 0.3 fusion.53
  478.1 0.3 fusion.52
  478.3 0.3 convolution_subtract_fusion.6
  478.6 0.3 fusion.50
  478.9 0.3 convolution_subtract_fusion.2
  479.2 0.3 fusion.48
  479.4 0.4 convolution_subtract_fusion.1
  479.8 0.3 fusion.47
  480.1 0.6 fusion.61
  (49 shorter events, 2.5 us)
Async XLA Ops:
  6.5 2.5 copy-start
  6.5 306.3 %all-reduce.3.cloned.1.call-start = ((), (), s32[]{:S(2)}) async-start(), calls=%async_computation.1 | async-start | bytes 3145728 | tf_op jit(solution)/shard_map/psum | solution.py:58
  9.1 3.0 copy-start.4
  11.8 2.4 copy-start.5
  322.1 1.0 copy-start.3
  369.7 1.0 copy-start.1
  471.1 4.9 copy-start.2
Sparse Core Ops, SparseCore 0:
  59.5 253.3 all-reduce.2

commit v2 on v1

--- a/solution.py
+++ b/solution.py
@@ -44,21 +44,28 @@
     train_sketch = sketch_terms(train_hidden, train_outgrad, train_mask, proj_in, proj_out)
     query_sketch = sketch_terms(query_hidden, query_outgrad, query_mask, proj_in, proj_out)
     block_rows = train_sketch.shape[0]
-    query_rows = query_sketch.shape[0]
-    devices = lax.axis_size(AXES)
-    width = train_sketch.shape[1]
-    chunk = width // devices
-    rows = jnp.concatenate([train_sketch, query_sketch], axis=0)
-    pieces = rows.reshape(block_rows + query_rows, devices, chunk).transpose(1, 0, 2)
-    gathered = lax.all_to_all(pieces, AXES, 0, 0, tiled=True)
-    train_cols = gathered[:, :block_rows, :].reshape(devices * block_rows, chunk)
-    query_cols = gathered[:, block_rows:, :].reshape(devices * query_rows, chunk)
-    both_cols = jnp.concatenate([train_cols, query_cols], axis=0)
-    partial = jnp.dot(train_cols, both_cols.T, precision=lax.Precision.HIGHEST)
-    summed = lax.psum(partial, AXES)
-    total_rows = devices * block_rows
-    gram_matrix = summed[:, :total_rows]
-    products = summed[:, total_rows:]
+    query_block = query_sketch.shape[0]
+    outer = lax.axis_size("train")
+    inner = lax.axis_size("query")
+    group_rows = lax.all_gather(train_sketch, "query", axis=0, tiled=True)
+    both = jnp.concatenate([train_sketch, query_sketch], axis=0)
+    column_rows = lax.all_gather(both, "train", axis=0, tiled=False)
+    column_rows = column_rows.reshape(outer * (block_rows + query_block), -1)
+    block = jnp.dot(group_rows, column_rows.T, precision=lax.Precision.HIGHEST)
+    blocks = lax.all_gather(block, AXES, axis=0, tiled=False)
+    group = inner * block_rows
+    blocks = blocks.reshape(outer, inner, group, outer, block_rows + query_block)
+    gram_matrix = (
+        blocks[..., :block_rows]
+        .transpose(0, 2, 3, 1, 4)
+        .reshape(outer * group, outer * inner * block_rows)
+    )
+    products = (
+        blocks[..., block_rows:]
+        .transpose(0, 2, 3, 1, 4)
+        .reshape(outer * group, outer * inner * query_block)
+    )
+    total_rows = gram_matrix.shape[0]
     damping = damping_share * jnp.trace(gram_matrix) / total_rows
     system = gram_matrix + damping * jnp.eye(total_rows, dtype=jnp.float32)
     factor = jnp.linalg.cholesky(system)

time: 493 us -> 409 us (0.83)
  waiting for transfers between devices: 254 us -> 111 us
  local copies, waits for them, and re-layouts: 22 us -> 60.7 us
  blocking collectives: 36.3 us -> 49.9 us
    psum x1 -> x0, waiting for transfers between devices: 254 us -> none  [body(): summed = lax.psum(partial, AXES)]
    all_gather x0 -> x1, waiting for transfers between devices: none -> 111 us  [body(): blocks = lax.all_gather(block, AXES, axis=0, tiled=False)]
    all_gather x0 -> x2, blocking collectives: none -> 49.9 us  [the longest x1 29.9 us: body(): column_rows = lax.all_gather(both, 'train', axis=0, tiled=False)]
    all_to_all x1 -> x0, blocking collectives: 36.3 us -> none  [body(): gathered = lax.all_to_all(pieces, AXES, 0, 0, tiled=True)]
    another operation x20 -> x32, local copies, waits for them, and re-layouts: 14.4 us -> 26.2 us
    reshape x2 -> x4, local copies, waits for them, and re-layouts: 0.15 us -> 10.2 us  [the longest x1 5.15 us: body(): blocks.reshape(outer, inner, group, outer, block_rows + query_block)]
    transpose x1 -> x3, local copies, waits for them, and re-layouts: 0.27 us -> 8.97 us  [the longest x2 5.89 us: body(): gram_matrix = blocks[..., :block_rows].transpose(0, 2, 3, 1, 4).reshape(o...]
    another operation x3 -> x4, other arithmetic: 42.5 us -> 43 us  [chol_solve(): lax.linalg.triangular_solve(factor, lower_solved, left_side=True, lower=T...]
where the time goes in v2:
time: 409 us; the launch traced here: 401 us
  other arithmetic  131 us (32%)
  waiting for transfers between devices  111 us (27%)
  local copies, waits for them, and re-layouts  60.7 us (15%)
  blocking collectives  49.9 us (12%)
  matrix products  30.6 us (7%)
  between operations  17.1 us (4%)
    all_gather x1, waiting for transfers between devices, body(): blocks = lax.all_gather(block, AXES, axis=0, tiled=False)  111 us
    another operation x14, other arithmetic, body(): factor = jnp.linalg.cholesky(system)  78.8 us
    another operation x4, other arithmetic, chol_solve(): lax.linalg.triangular_solve(factor, lower_solved, left_side=True, lower=T...  43 us
    all_gather x1, blocking collectives, body(): column_rows = lax.all_gather(both, 'train', axis=0, tiled=False)  29.9 us
    all_gather x1, blocking collectives, body(): group_rows = lax.all_gather(train_sketch, 'query', axis=0, tiled=True)  20 us
    another operation x20, local copies, waits for them, and re-layouts  14.5 us
    another operation x12, local copies, waits for them, and re-layouts, chol_solve(): lax.linalg.triangular_solve(factor, right, left_side=True, lower=True)  11.7 us
  transfers between devices with their start and end apart: 1, of which 1 were waited for; matrix products, arithmetic and copies ran while one was open for 0% of the time, Pallas kernels for 0%

profile of v2, /device:TPU:1, one launch (start us, length us, event | category | flops | bytes accessed | tf_op | source)
XLA Modules:
  0.0 401.0 jit_solution(15269098705152057471)
XLA Ops:
  6.5 0.8 convert_element_type.23
  7.5 5.1 %convolution_multiply_fusion = f32[192,64]{0,1:T(8,128)S(1)} fusion(bf16[192,14336]{1,0:T(8,128)(2,1)} %bitcast.104, bf16[14336,64]{0,1:T(8,128)(2,1)} %param.15, f32[192]{0:T(256)S(1)} %convert_element_type.24), kind=kOutput, calls=%fused_computation.18 | convolution fusion | flops 352333824 | bytes 7389952 | tf_op jit(solution)/shard_map/dot_general | solution.py:17
  12.6 2.1 fusion.8
  15.2 1.5 fusion.6
  16.7 2.6 fusion.2
  19.6 20.0 %all-gather.2 = f32[16,2,4096]{2,1,0:T(2,128)S(1)} all-gather(f32[1,2,4096]{2,1,0:T(2,128)S(1)} %reshape.159), channel_id=1, replica_groups=mesh['train'=16,'query'=16] {'query'}, dimensions={0}, use_global_device_ids=true | all-gather | bytes 557056 | tf_op jit(solution)/shard_map/all_gather | solution.py:50
  39.6 1.2 reshape.160
  40.8 29.9 %all-gather.3 = f32[16,3,4096]{2,1,0:T(4,128)} all-gather(f32[1,3,4096]{2,1,0:T(4,128)S(1)} %maximum_bitcast_fusion), channel_id=2, replica_groups=mesh['train'=16,'query'=16] {'train'}, dimensions={0}, use_global_device_ids=true | all-gather | bytes 835584 | tf_op jit(solution)/shard_map/all_gather | solution.py:52
  70.7 1.6 reshape.162
  72.3 2.4 fusion.64
  75.3 111.3 %all-gather.6.cloned.1.call-done = f32[8192,48]{1,0:T(8,128)} async-done(((f32[32,48]{1,0:T(8,128)}), f32[8192,48]{1,0:T(8,128)}) %all-gather.6.cloned.1.call-update) | async-done | bytes 1572880 | tf_op jit(solution)/shard_map/all_gather | solution.py:55
  186.6 3.7 copy.37
  190.3 5.2 %reshape.134 = f32[16,16,32,16,3]{2,1,0,4,3:T(8,128)} reshape(f32[8192,48]{0,1:T(8,128)} %copy.37) | data formatting | bytes 3145728 | tf_op jit(solution)/shard_map/reshape | solution.py:57
  195.4 3.1 slice_bitcast_fusion.1
  198.5 2.5 slice_bitcast_fusion
  201.1 3.3 copy.38
  204.4 4.8 %reshape.135 = f32[512,512]{0,1:T(8,128)} reshape(f32[16,32,16,16,2]{1,0,4,3,2:T(8,128)} %copy.38) | data formatting | bytes 2097152 | tf_op jit(solution)/shard_map/reshape | solution.py:61
  209.2 4.0 select_reduce_fusion
  213.8 2.4 select_add_fusion
  216.1 2.5 copy.39
  218.7 1.8 fusion.5
  220.5 1.0 copy-done.2
  221.5 11.7 %cholesky.103 = f32[128,128]{1,0:T(8,128)S(1)} custom-call(f32[128,128]{1,0:T(8,128)S(1)} %cholesky.263), custom_call_target="Cholesky" | custom-call | tf_op jit(solution)/shard_map/jit(cholesky)/cholesky | solution.py:71
  233.3 9.8 %custom-call.32 = f32[1,128,128]{1,2,0:T(8,128)S(1)} custom-call(f32[1,128,128]{2,1,0:T(8,128)S(1)} %get-tuple-element.44), custom_call_target="InvertDiagBlocksLowerTriangular" | custom-call | tf_op jit(solution)/shard_map/jit(cholesky)/cholesky | solution.py:71
  243.1 1.2 fusion.30
  244.4 1.3 convolution_subtract_fusion
  245.8 11.9 %cholesky.215 = f32[128,128]{1,0:T(8,128)S(1)} custom-call(f32[128,128]{1,0:T(8,128)S(1)} %cholesky.267), custom_call_target="Cholesky" | custom-call | tf_op jit(solution)/shard_map/jit(cholesky)/cholesky | solution.py:71
  257.8 9.8 %custom-call.33 = f32[1,128,128]{1,2,0:T(8,128)S(1)} custom-call(f32[1,128,128]{2,1,0:T(8,128)S(1)} %get-tuple-element.42), custom_call_target="InvertDiagBlocksLowerTriangular" | custom-call | tf_op jit(solution)/shard_map/jit(cholesky)/cholesky | solution.py:71
  268.1 1.0 copy-done.1
  269.1 1.5 convolution_subtract_fusion.5
  270.6 11.7 %cholesky.236 = f32[128,128]{1,0:T(8,128)S(1)} custom-call(f32[128,128]{1,0:T(8,128)S(1)} %cholesky.272), custom_call_target="Cholesky" | custom-call | tf_op jit(solution)/shard_map/jit(cholesky)/cholesky | solution.py:71
  282.5 0.6 constant_dynamic-update-slice_fusion.1
  283.1 9.8 %custom-call.34 = f32[1,128,128]{1,2,0:T(8,128)S(1)} custom-call(f32[1,128,128]{2,1,0:T(8,128)S(1)} %get-tuple-element.40), custom_call_target="InvertDiagBlocksLowerTriangular" | custom-call | tf_op jit(solution)/shard_map/jit(cholesky)/cholesky | solution.py:71
  292.9 0.9 convolution_dynamic-update-slice_fusion.1
  293.9 1.5 convolution_subtract_fusion.8
  295.4 11.9 %cholesky.253 = f32[128,128]{1,0:T(8,128)S(1)} custom-call(f32[128,128]{1,0:T(8,128)S(1)} %convolution_subtract_fusion.8), custom_call_target="Cholesky" | custom-call | tf_op jit(solution)/shard_map/jit(cholesky)/cholesky | solution.py:71
  307.3 0.7 copy.46
  308.1 2.7 fusion.62
  311.2 1.2 copy.53
  312.7 0.8 copy.54
  313.5 1.2 copy.51
  314.8 0.9 triangular_solve.181
  315.7 1.0 copy.52
  316.7 1.2 copy.49
  317.9 0.9 triangular_solve.172
  318.8 1.0 copy.50
  319.8 0.7 compare_reduce_fusion.1
  320.5 0.6 compare_reduce_fusion
  321.1 1.5 constant_dynamic-update-slice_fusion.2
  322.6 0.7 compare_reduce_fusion.2
  325.8 2.4 select_select_fusion
  328.8 14.5 %while.1 = (s32[]{:T(128)}, f32[512,512]{0,1:T(8,128)}, s32[4,2]{0,1:T(2,128)S(1)}, f32[4,128,128]{2,1,0:T(8,128)}, s32[]{:T(128)}) while((s32[]{:T(128)}, f32[512,512]{0,1:T(8,128)}, s32[4,2]{0,1:T(2,128)S(1)}, f32[4,128,128]{2,1,0:T(8,128)}, s32[]{:T(128)}) %tuple.29), condition=%wide.while_cond, body=%wide.while_body.sunk | while | flops 2 | bytes 393329 | solution.py:29
  329.5 2.2 dynamic-slice.7
  333.1 2.2 dynamic-slice.7
  336.8 2.2 dynamic-slice.7
  340.4 2.2 dynamic-slice.7
  342.7 0.6 bitcast_dynamic-update-slice_fusion.2
  343.3 40.1 %custom-call.35 = f32[4,128,128]{1,2,0:T(8,128)S(1)} custom-call(f32[4,128,128]{2,1,0:T(8,128)} %get-tuple-element.12), custom_call_target="InvertDiagBlocksLowerTriangular" | custom-call | tf_op jit(solution)/shard_map/triangular_solve | solution.py:29
  383.8 1.1 convolution_subtract_fusion.7
  385.3 1.3 convolution_subtract_fusion.4
  386.9 1.4 convolution_subtract_fusion.3
  388.9 1.1 convolution_subtract_fusion.6
  390.3 1.2 convolution_subtract_fusion.2
  391.8 1.3 convolution_subtract_fusion.1
  (68 shorter events, 11.6 us)
Async XLA Ops:
  6.5 10.2 %copy-start = (bf16[1,96,14336]{2,1,0:T(8,128)(2,1)S(1)}, bf16[1,96,14336]{2,1,0:T(8,128)(2,1)}, u32[]{:S(2)}) copy-start(bf16[1,96,14336]{2,1,0:T(8,128)(2,1)} %param.12) | copy-start | bytes 8257540
  6.5 180.0 %all-gather.6.cloned.1.call-start = ((), (), s32[]{:S(2)}) async-start(), calls=%async_computation | async-start | bytes 4210688 | tf_op jit(solution)/shard_map/all_gather | solution.py:55
  7.5 5.2 %copy-start.3 = (bf16[4096,64]{0,1:T(8,128)(2,1)S(1)}, bf16[4096,64]{0,1:T(8,128)(2,1)}, u32[]{:S(2)}) copy-start(bf16[4096,64]{0,1:T(8,128)(2,1)} %param.14) | copy-start | bytes 1572868
  7.5 7.7 %copy-start.5 = (s32[1,96]{1,0:T(1,128)S(1)}, s32[1,96]{1,0:T(1,128)}, u32[]{:S(2)}) copy-start(s32[1,96]{1,0:T(1,128)} %param.13) | copy-start | bytes 1156
  220.5 1.0 copy-start.2
  268.1 1.0 copy-start.1
  325.8 61.1 %copy-start.4 = (f32[128,256]{1,0:T(8,128)S(1)}, f32[128,256]{1,0:T(8,128)}, u32[]{:S(2)}) copy-start(f32[128,256]{1,0:T(8,128)} %copy.54) | copy-start | bytes 393220
Sparse Core Ops, SparseCore 0:
  74.9 111.6 all-gather.5

commit v3 on v1

v3 whole, which is shorter than its diff:
```python
import jax
import jax.numpy as jnp
from jax import lax
from jax.sharding import PartitionSpec as P

damping_share = 0.1
AXES = ("train", "query")
HIGHEST = lax.Precision.HIGHEST


def sketch_terms(hidden, outgrad, mask, proj_in, proj_out):
    proof_count, token_count, model_width = hidden.shape
    input_side = jnp.dot(
        hidden.reshape(proof_count * token_count, model_width),
        proj_in,
        preferred_element_type=jnp.float32,
    )
    output_side = jnp.dot(
        outgrad.reshape(proof_count * token_count, -1), proj_out, preferred_element_type=jnp.float32
    )
    output_side = output_side * mask.reshape(-1, 1).astype(jnp.float32)
    input_side = input_side.reshape(proof_count, token_count, -1)
    output_side = output_side.reshape(proof_count, token_count, -1)
    outer_sum = jnp.einsum("pti,ptj->pij", output_side, input_side, precision=HIGHEST)
    return outer_sum.reshape(proof_count, -1)


def spd_solve(system, right, tolerance=1e-3, most_steps=48):
    size = system.shape[0]
    diagonal = jnp.diagonal(system)
    inv_sqrt = lax.rsqrt(diagonal)
    bound = jnp.max(jnp.sum(jnp.abs(system) * inv_sqrt[:, None] * inv_sqrt[None, :], axis=1))
    eye = jnp.eye(size, dtype=system.dtype)
    start = eye * (1.0 / (diagonal * bound))[None, :]

    def going(carry):
        step, _, residual = carry
        return (step < most_steps) & (residual > tolerance)

    def advance(carry):
        step, inverse, _ = carry
        remainder = eye - jnp.dot(system, inverse, precision=HIGHEST)
        residual = jnp.max(jnp.abs(remainder))
        return step + 1, inverse + jnp.dot(inverse, remainder, precision=HIGHEST), residual

    _, inverse, _ = lax.while_loop(
        going, advance, (jnp.int32(0), start, jnp.array(jnp.inf, system.dtype))
    )
    solved = jnp.dot(inverse, right, precision=HIGHEST)
    return solved + jnp.dot(
        inverse, right - jnp.dot(system, solved, precision=HIGHEST), precision=HIGHEST
    )


def body(
    train_hidden,
    train_outgrad,
    train_mask,
    query_hidden,
    query_outgrad,
    query_mask,
    proj_in,
    proj_out,
):
    train_sketch = sketch_terms(train_hidden, train_outgrad, train_mask, proj_in, proj_out)
    query_sketch = sketch_terms(query_hidden, query_outgrad, query_mask, proj_in, proj_out)
    block_rows = train_sketch.shape[0]
    width = train_sketch.shape[1]
    both = jnp.concatenate([train_sketch, query_sketch], axis=0)
    everyone = lax.all_gather(both, AXES, axis=0, tiled=False)
    all_train = everyone[:, :block_rows].reshape(-1, width)
    all_queries = everyone[:, block_rows:].reshape(-1, width)
    gram_matrix = jnp.dot(all_train, all_train.T, precision=HIGHEST)
    products = jnp.dot(all_train, all_queries.T, precision=HIGHEST)
    total_rows = gram_matrix.shape[0]
    damping = damping_share * jnp.trace(gram_matrix) / total_rows
    system = gram_matrix + damping * jnp.eye(total_rows, dtype=jnp.float32)
    solved = total_rows * spd_solve(system, products)
    return lax.dynamic_slice_in_dim(
        solved, lax.axis_index(AXES) * block_rows, block_rows, 0
    )


def solution(mesh):
    in_specs = (
        P(AXES, None, None),
        P(AXES, None, None),
        P(AXES, None),
        P(AXES, None, None),
        P(AXES, None, None),
        P(AXES, None),
        P(),
        P(),
    )
    out_specs = P(AXES, None)
    return jax.shard_map(body, mesh=mesh, in_specs=in_specs, out_specs=out_specs, check_vma=False)
```

time: 493 us -> 318 us (0.65)
  waiting for transfers between devices: 254 us -> 130 us
  other arithmetic: 129 us -> 8.92 us
  matrix products: 30 us -> 106 us
  blocking collectives: 36.3 us -> 0 us
  local copies, waits for them, and re-layouts: 22 us -> 51.5 us
  loops' own time: 0.05 us -> 6.25 us
    psum x1 -> x0, waiting for transfers between devices: 254 us -> none  [body(): summed = lax.psum(partial, AXES)]
    all_gather x0 -> x1, waiting for transfers between devices: none -> 130 us  [body(): everyone = lax.all_gather(both, AXES, axis=0, tiled=False)]
    another operation x17 -> x0, other arithmetic: 121 us -> none  [the longest x14 78.8 us: body(): factor = jnp.linalg.cholesky(system)]
    dot_general x3 -> x25, matrix products: 2.98 us -> 94.5 us  [the longest x9 34.1 us: advance(): remainder = eye - jnp.dot(system, inverse, precision=HIGHEST)]
    all_to_all x1 -> x0, blocking collectives: 36.3 us -> none  [body(): gathered = lax.all_to_all(pieces, AXES, 0, 0, tiled=True)]
    slice x2, local copies, waits for them, and re-layouts: 0.24 us -> 17.8 us  [the longest x1 9.92 us: body(): all_train = everyone[:, :block_rows].reshape(-1, width)]
    another operation x34 -> x0, local copies, waits for them, and re-layouts: 16.4 us -> none
    another operation x20 -> x0, matrix products: 15.6 us -> none  [the longest x7 6.86 us: chol_solve(): lax.linalg.triangular_solve(factor, right, left_side=True, lower=True)]
where the time goes in v3:
time: 318 us; the launch traced here: 316 us
  waiting for transfers between devices  130 us (41%)
  matrix products  106 us (33%)
  local copies, waits for them, and re-layouts  51.5 us (16%)
  between operations  14.3 us (4%)
  other arithmetic  8.92 us (3%)
  loops' own time  6.25 us (2%)
    all_gather x1, waiting for transfers between devices, body(): everyone = lax.all_gather(both, AXES, axis=0, tiled=False)  130 us
    dot_general x9, matrix products, advance(): remainder = eye - jnp.dot(system, inverse, precision=HIGHEST)  34.1 us
    dot_general x9, matrix products, advance(): jnp.dot(inverse, remainder, precision=HIGHEST)  25.5 us
    dot_general x1, matrix products, body(): gram_matrix = jnp.dot(all_train, all_train.T, precision=HIGHEST)  18.1 us
    while x9, local copies, waits for them, and re-layouts  11 us
    reshape x1, local copies, waits for them, and re-layouts, body(): all_train = everyone[:, :block_rows].reshape(-1, width)  10.9 us
    slice x1, local copies, waits for them, and re-layouts, body(): all_train = everyone[:, :block_rows].reshape(-1, width)  9.92 us
    gather x1, local copies, waits for them, and re-layouts, spd_solve(): diagonal = jnp.diagonal(system)  8.42 us
  transfers between devices with their start and end apart: 1, of which 1 were waited for; matrix products, arithmetic and copies ran while one was open for 0% of the time, Pallas kernels for 0%

profile of v3, /device:TPU:1, one launch (start us, length us, event | category | flops | bytes accessed | tf_op | source)
XLA Modules:
  0.0 316.4 jit_solution(12667484423947901876)
XLA Ops:
  6.5 0.0 copy-start
  6.5 0.0 all-gather.4.cloned.1.call-start
  6.5 0.8 convert_bitcast_fusion
  7.3 0.7 convert_element_type.26
  8.1 0.1 convert_element_type.27
  8.1 1.7 fusion.12
  9.8 2.6 fusion.8
  12.5 0.2 fusion.19
  12.6 0.1 reshape.69
  12.7 0.0 copy-start.3
  12.8 5.1 %convolution_multiply_fusion = f32[192,64]{0,1:T(8,128)S(1)} fusion(bf16[192,14336]{1,0:T(8,128)(2,1)} %bitcast.58, bf16[14336,64]{0,1:T(8,128)(2,1)} %param.17, f32[192]{0:T(256)S(1)} %convert_element_type.27), kind=kOutput, calls=%fused_computation.13 | convolution fusion | flops 352333824 | bytes 7389952 | tf_op jit(solution)/shard_map/dot_general | solution.py:18
  17.8 0.1 reshape.65
  17.9 2.1 fusion.14
  20.0 0.2 fusion.16
  20.3 0.1 reshape.66
  20.4 0.7 maximum_bitcast_fusion
  21.0 0.0 all-gather.4.cloned.1.call-update
  21.1 129.6 %all-gather.4.cloned.1.call-done = f32[256,3,4096]{2,1,0:T(4,128)} async-done(((f32[1,3,4096]{2,1,0:T(4,128)}), f32[256,3,4096]{2,1,0:T(4,128)}) %all-gather.4.cloned.1.call-update) | async-done | bytes 12582928 | tf_op jit(solution)/shard_map/all_gather | solution.py:70
  150.6 9.9 %slice.10 = f32[256,2,4096]{2,1,0:T(2,128)} slice(f32[256,3,4096]{2,1,0:T(4,128)} %all-gather.4.cloned.1.call-done), slice={[0:256], [0:2], [0:4096]} | slice | bytes 16777216 | tf_op jit(solution)/shard_map/slice | solution.py:71
  160.5 10.9 %reshape.70 = f32[512,4096]{1,0:T(8,128)} reshape(f32[256,2,4096]{2,1,0:T(2,128)} %slice.10) | data formatting | bytes 16777216 | tf_op jit(solution)/shard_map/reshape | solution.py:71
  171.4 18.1 %select_reduce_fusion = (f32[]{:T(128)}, f32[512,512]{0,1:T(8,128)}) fusion(f32[512,4096]{1,0:T(8,128)} %reshape.70), kind=kOutput, calls=%fused_computation.17 | convolution fusion | flops 12885688320 | bytes 9437188 | tf_op jit(solution)/shard_map/dot_general | solution.py:73
  189.5 7.9 %slice.11 = f32[256,1,4096]{2,1,0:T(1,128)S(1)} slice(f32[256,3,4096]{2,1,0:T(4,128)} %all-gather.4.cloned.1.call-done), slice={[0:256], [2:3], [0:4096]} | slice | bytes 8388608 | tf_op jit(solution)/shard_map/slice | solution.py:72
  197.4 0.4 copy-done.1
  197.7 8.4 %fusion.3 = f32[512,256]{1,0:T(8,128)S(1)} fusion(f32[512,4096]{1,0:T(8,128)S(1)} %copy-done.1, f32[256,1,4096]{2,1,0:T(1,128)S(1)} %slice.11), kind=kOutput, calls=%fused_computation.7 | convolution fusion | flops 6442450944 | bytes 13107200 | tf_op jit(solution)/shard_map/dot_general | solution.py:74
  206.8 2.3 select_add_fusion
  209.2 2.6 copy.14
  211.8 8.4 %gather_fusion = f32[512]{0:T(512)S(1)} fusion(f32[512,512]{0,1:T(8,128)} %select_add_fusion, s32[512]{0:T(512)S(1)} %bitcast.57), kind=kCustom, calls=%fused_computation | custom fusion | bytes 8192 | tf_op jit(solution)/shard_map/jit(diagonal)/cond/branch_0_fun/gather | solution.py:30
  220.2 1.4 multiply_reduce_fusion
  221.7 0.6 reduce_max.18
  222.3 0.6 multiply_divide_fusion
  222.9 1.2 fusion.11
  224.0 76.9 %while.13 = (s32[]{:T(128)}, f32[512,512]{0,1:T(8,128)}, f32[]{:T(128)}, f32[512,512]{1,0:T(8,128)}, s32[]{:T(128)}) while((s32[]{:T(128)}, f32[512,512]{0,1:T(8,128)}, f32[]{:T(128)}, f32[512,512]{1,0:T(8,128)}, s32[]{:T(128)}) %tuple.28), condition=%wide.region_5.6_spmd.clone, body=%wide.region_3.5_spmd.clone.sunk | while | flops 3222798336 | bytes 8388685 | solution.py:46
  224.1 1.2 copy.35
  225.3 3.8 %abs_reduce_fusion.2 = (f32[]{:T(128)}, f32[512,512]{1,0:T(8,128)S(1)}) fusion(f32[512,512]{1,0:T(8,128)} %get-tuple-element.108, f32[512,512]{0,1:T(8,128)S(1)} %copy.35), kind=kOutput, calls=%fused_computation.6.clone.1 | convolution fusion | flops 1611923456 | bytes 3145732 | tf_op jit(solution)/shard_map/while/body/dot_general | solution.py:42
  229.1 2.8 fusion.52
  232.6 1.2 copy.35
  233.8 3.8 %abs_reduce_fusion.2 = (f32[]{:T(128)}, f32[512,512]{1,0:T(8,128)S(1)}) fusion(f32[512,512]{1,0:T(8,128)} %get-tuple-element.108, f32[512,512]{0,1:T(8,128)S(1)} %copy.35), kind=kOutput, calls=%fused_computation.6.clone.1 | convolution fusion | flops 1611923456 | bytes 3145732 | tf_op jit(solution)/shard_map/while/body/dot_general | solution.py:42
  237.6 2.8 fusion.52
  241.1 1.2 copy.35
  242.4 3.8 %abs_reduce_fusion.2 = (f32[]{:T(128)}, f32[512,512]{1,0:T(8,128)S(1)}) fusion(f32[512,512]{1,0:T(8,128)} %get-tuple-element.108, f32[512,512]{0,1:T(8,128)S(1)} %copy.35), kind=kOutput, calls=%fused_computation.6.clone.1 | convolution fusion | flops 1611923456 | bytes 3145732 | tf_op jit(solution)/shard_map/while/body/dot_general | solution.py:42
  246.2 2.8 fusion.52
  249.7 1.2 copy.35
  250.9 3.8 %abs_reduce_fusion.2 = (f32[]{:T(128)}, f32[512,512]{1,0:T(8,128)S(1)}) fusion(f32[512,512]{1,0:T(8,128)} %get-tuple-element.108, f32[512,512]{0,1:T(8,128)S(1)} %copy.35), kind=kOutput, calls=%fused_computation.6.clone.1 | convolution fusion | flops 1611923456 | bytes 3145732 | tf_op jit(solution)/shard_map/while/body/dot_general | solution.py:42
  254.7 2.8 fusion.52
  258.2 1.2 copy.35
  259.5 3.8 %abs_reduce_fusion.2 = (f32[]{:T(128)}, f32[512,512]{1,0:T(8,128)S(1)}) fusion(f32[512,512]{1,0:T(8,128)} %get-tuple-element.108, f32[512,512]{0,1:T(8,128)S(1)} %copy.35), kind=kOutput, calls=%fused_computation.6.clone.1 | convolution fusion | flops 1611923456 | bytes 3145732 | tf_op jit(solution)/shard_map/while/body/dot_general | solution.py:42
  263.2 2.8 fusion.52
  266.8 1.2 copy.35
  268.0 3.8 %abs_reduce_fusion.2 = (f32[]{:T(128)}, f32[512,512]{1,0:T(8,128)S(1)}) fusion(f32[512,512]{1,0:T(8,128)} %get-tuple-element.108, f32[512,512]{0,1:T(8,128)S(1)} %copy.35), kind=kOutput, calls=%fused_computation.6.clone.1 | convolution fusion | flops 1611923456 | bytes 3145732 | tf_op jit(solution)/shard_map/while/body/dot_general | solution.py:42
  271.8 2.8 fusion.52
  275.3 1.2 copy.35
  276.6 3.8 %abs_reduce_fusion.2 = (f32[]{:T(128)}, f32[512,512]{1,0:T(8,128)S(1)}) fusion(f32[512,512]{1,0:T(8,128)} %get-tuple-element.108, f32[512,512]{0,1:T(8,128)S(1)} %copy.35), kind=kOutput, calls=%fused_computation.6.clone.1 | convolution fusion | flops 1611923456 | bytes 3145732 | tf_op jit(solution)/shard_map/while/body/dot_general | solution.py:42
  280.3 2.8 fusion.52
  283.9 1.2 copy.35
  285.1 3.8 %abs_reduce_fusion.2 = (f32[]{:T(128)}, f32[512,512]{1,0:T(8,128)S(1)}) fusion(f32[512,512]{1,0:T(8,128)} %get-tuple-element.108, f32[512,512]{0,1:T(8,128)S(1)} %copy.35), kind=kOutput, calls=%fused_computation.6.clone.1 | convolution fusion | flops 1611923456 | bytes 3145732 | tf_op jit(solution)/shard_map/while/body/dot_general | solution.py:42
  288.9 2.8 fusion.52
  292.4 1.2 copy.35
  293.6 3.8 %abs_reduce_fusion.2 = (f32[]{:T(128)}, f32[512,512]{1,0:T(8,128)S(1)}) fusion(f32[512,512]{1,0:T(8,128)} %get-tuple-element.108, f32[512,512]{0,1:T(8,128)S(1)} %copy.35), kind=kOutput, calls=%fused_computation.6.clone.1 | convolution fusion | flops 1611923456 | bytes 3145732 | tf_op jit(solution)/shard_map/while/body/dot_general | solution.py:42
  297.4 2.8 fusion.52
  301.0 0.0 copy-start.2
  301.0 3.1 fusion.20
  304.1 3.0 convolution_subtract_fusion.1
  307.2 1.8 fusion.21
  309.0 0.6 fusion.18
  (6 shorter events, 0.0 us)
Async XLA Ops:
  6.5 3.3 %copy-start = (bf16[1,96,14336]{2,1,0:T(8,128)(2,1)S(1)}, bf16[1,96,14336]{2,1,0:T(8,128)(2,1)}, u32[]{:S(2)}) copy-start(bf16[1,96,14336]{2,1,0:T(8,128)(2,1)} %param.14) | copy-start | bytes 8257540
  6.5 144.1 %all-gather.4.cloned.1.call-start = ((), (), s32[]{:S(2)}) async-start(), calls=%async_computation | async-start | bytes 16842752 | tf_op jit(solution)/shard_map/all_gather | solution.py:70
  12.7 5.2 %copy-start.3 = (bf16[4096,64]{0,1:T(8,128)(2,1)S(1)}, bf16[4096,64]{0,1:T(8,128)(2,1)}, u32[]{:S(2)}) copy-start(bf16[4096,64]{0,1:T(8,128)(2,1)} %param.16) | copy-start | bytes 1572868
  189.5 8.3 %copy-start.1 = (f32[512,4096]{1,0:T(8,128)S(1)}, f32[512,4096]{1,0:T(8,128)}, u32[]{:S(2)}) copy-start(f32[512,4096]{1,0:T(8,128)} %reshape.70) | copy-start | bytes 25165828
  301.0 6.2 %copy-start.2 = (f32[512,512]{0,1:T(8,128)S(1)}, f32[512,512]{0,1:T(8,128)}, u32[]{:S(2)}) copy-start(f32[512,512]{0,1:T(8,128)} %get-tuple-element.32) | copy-start | bytes 3145732
Sparse Core Ops, SparseCore 0:
  21.2 129.4 all-gather.3

commit v4 on v3

--- a/solution.py
+++ b/solution.py
@@ -25,27 +25,32 @@
     return outer_sum.reshape(proof_count, -1)
 
 
-def spd_solve(system, right, tolerance=1e-3, most_steps=48):
+def spd_solve(system, right, coarse_until=1e-2, tolerance=1e-3, most_steps=48):
     size = system.shape[0]
-    diagonal = jnp.diagonal(system)
+    eye = jnp.eye(size, dtype=system.dtype)
+    diagonal = jnp.sum(system * eye, axis=1)
     inv_sqrt = lax.rsqrt(diagonal)
     bound = jnp.max(jnp.sum(jnp.abs(system) * inv_sqrt[:, None] * inv_sqrt[None, :], axis=1))
-    eye = jnp.eye(size, dtype=system.dtype)
     start = eye * (1.0 / (diagonal * bound))[None, :]
 
-    def going(carry):
-        step, _, residual = carry
-        return (step < most_steps) & (residual > tolerance)
+    def stepper(precision):
+        def advance(carry):
+            step, inverse, _ = carry
+            remainder = eye - jnp.dot(system, inverse, precision=precision)
+            residual = jnp.sqrt(jnp.sum(remainder * remainder))
+            return step + 1, inverse + jnp.dot(inverse, remainder, precision=precision), residual
+        return advance
 
-    def advance(carry):
-        step, inverse, _ = carry
-        remainder = eye - jnp.dot(system, inverse, precision=HIGHEST)
-        residual = jnp.max(jnp.abs(remainder))
-        return step + 1, inverse + jnp.dot(inverse, remainder, precision=HIGHEST), residual
+    def until(level):
+        def going(carry):
+            step, _, residual = carry
+            return (step < most_steps) & (residual > level)
+        return going
 
-    _, inverse, _ = lax.while_loop(
-        going, advance, (jnp.int32(0), start, jnp.array(jnp.inf, system.dtype))
-    )
+    carry = (jnp.int32(0), start, jnp.array(jnp.inf, system.dtype))
+    carry = lax.while_loop(until(coarse_until), stepper(lax.Precision.HIGH), carry)
+    carry = (carry[0], carry[1], jnp.array(jnp.inf, system.dtype))
+    _, inverse, _ = lax.while_loop(until(tolerance), stepper(HIGHEST), carry)
     solved = jnp.dot(inverse, right, precision=HIGHEST)
     return solved + jnp.dot(
         inverse, right - jnp.dot(system, solved, precision=HIGHEST), precision=HIGHEST
@@ -65,19 +70,22 @@
     train_sketch = sketch_terms(train_hidden, train_outgrad, train_mask, proj_in, proj_out)
     query_sketch = sketch_terms(query_hidden, query_outgrad, query_mask, proj_in, proj_out)
     block_rows = train_sketch.shape[0]
-    width = train_sketch.shape[1]
     both = jnp.concatenate([train_sketch, query_sketch], axis=0)
-    everyone = lax.all_gather(both, AXES, axis=0, tiled=False)
-    all_train = everyone[:, :block_rows].reshape(-1, width)
-    all_queries = everyone[:, block_rows:].reshape(-1, width)
+    everyone = lax.all_gather(both[:, None, :], AXES, axis=1, tiled=True)
+    devices = everyone.shape[1]
+    all_train = everyone[:block_rows].reshape(block_rows * devices, -1)
+    all_queries = everyone[block_rows:].reshape(-1, everyone.shape[2])
     gram_matrix = jnp.dot(all_train, all_train.T, precision=HIGHEST)
     products = jnp.dot(all_train, all_queries.T, precision=HIGHEST)
     total_rows = gram_matrix.shape[0]
-    damping = damping_share * jnp.trace(gram_matrix) / total_rows
-    system = gram_matrix + damping * jnp.eye(total_rows, dtype=jnp.float32)
+    eye = jnp.eye(total_rows, dtype=jnp.float32)
+    damping = damping_share * jnp.sum(gram_matrix * eye) / total_rows
+    system = gram_matrix + damping * eye
     solved = total_rows * spd_solve(system, products)
-    return lax.dynamic_slice_in_dim(
-        solved, lax.axis_index(AXES) * block_rows, block_rows, 0
+    me = lax.axis_index(AXES)
+    return jnp.concatenate(
+        [lax.dynamic_slice_in_dim(solved, r * devices + me, 1, 0) for r in range(block_rows)],
+        axis=0,
     )
 
 

time: 318 us -> 387 us (1.22)
  local copies, waits for them, and re-layouts: 51.5 us -> 101 us
  matrix products: 106 us -> 126 us
    slice x2, local copies, waits for them, and re-layouts: 17.8 us -> 57.2 us  [the longest x1 47.3 us: body(): all_queries = everyone[block_rows:].reshape(-1, everyone.shape[2])]
    dot_general x18 -> x20, matrix products: 59.6 us -> 78.5 us  [the longest x10 39.4 us: advance(): jnp.dot(inverse, remainder, precision=precision)]
    while x9 -> x30, local copies, waits for them, and re-layouts: 11 us -> 22.1 us
    gather x1 -> x0, local copies, waits for them, and re-layouts: 8.42 us -> none  [spd_solve(): diagonal = jnp.diagonal(system)]
    reshape x1 -> x2, local copies, waits for them, and re-layouts: 10.9 us -> 18.7 us  [the longest x1 13.8 us: body(): all_train = everyone[:block_rows].reshape(block_rows * devices, -1)]
where the time goes in v4:
time: 387 us; the launch traced here: 386 us
  waiting for transfers between devices  130 us (34%)
  matrix products  126 us (33%)
  local copies, waits for them, and re-layouts  101 us (26%)
  between operations  14.2 us (4%)
  other arithmetic  8.88 us (2%)
  loops' own time  6.66 us (2%)
    all_gather x1, waiting for transfers between devices, body(): everyone = lax.all_gather(both[:, None, :], AXES, axis=1, tiled=True)  130 us
    slice x1, local copies, waits for them, and re-layouts, body(): all_queries = everyone[block_rows:].reshape(-1, everyone.shape[2])  47.3 us
    dot_general x10, matrix products, advance(): jnp.dot(inverse, remainder, precision=precision)  39.4 us
    dot_general x10, matrix products, advance(): remainder = eye - jnp.dot(system, inverse, precision=precision)  39.2 us
    while x30, local copies, waits for them, and re-layouts  22.1 us
    dot_general x1, matrix products, body(): gram_matrix = jnp.dot(all_train, all_train.T, precision=HIGHEST)  18.1 us
    reshape x1, local copies, waits for them, and re-layouts, body(): all_train = everyone[:block_rows].reshape(block_rows * devices, -1)  13.8 us
    slice x1, local copies, waits for them, and re-layouts, body(): all_train = everyone[:block_rows].reshape(block_rows * devices, -1)  9.87 us
  transfers between devices with their start and end apart: 1, of which 1 were waited for; matrix products, arithmetic and copies ran while one was open for 0% of the time, Pallas kernels for 0%

profile of v4, /device:TPU:1, one launch (start us, length us, event | category | flops | bytes accessed | tf_op | source)
XLA Modules:
  0.0 386.0 jit_solution(5797291487552783281)
XLA Ops:
  6.5 0.8 convert_bitcast_fusion
  7.3 0.7 convert_element_type.28
  8.1 1.6 fusion.13
  9.8 2.4 fusion.9
  12.5 5.1 %convolution_multiply_fusion = f32[192,64]{0,1:T(8,128)S(1)} fusion(bf16[192,14336]{1,0:T(8,128)(2,1)} %bitcast.70, bf16[14336,64]{0,1:T(8,128)(2,1)} %param.19, f32[192]{0:T(256)S(1)} %convert_element_type.29), kind=kOutput, calls=%fused_computation.18 | convolution fusion | flops 352333824 | bytes 7389952 | tf_op jit(solution)/shard_map/dot_general | solution.py:18
  17.7 2.1 fusion.15
  20.1 0.7 pad_maximum_fusion
  20.8 129.6 %all-gather.3.cloned.1.call-done = f32[3,1048576]{1,0:T(4,128)} async-done(((f32[3,4096]{1,0:T(4,128)}), f32[3,1048576]{1,0:T(4,128)}) %all-gather.3.cloned.1.call-update) | async-done | bytes 12582928 | tf_op jit(solution)/shard_map/all_gather | solution.py:74
  150.4 9.9 %slice.10 = f32[2,1048576]{1,0:T(2,128)} slice(f32[3,1048576]{1,0:T(4,128)} %all-gather.3.cloned.1.call-done), slice={[0:2], [0:1048576]} | slice | bytes 16777216 | tf_op jit(solution)/shard_map/slice | solution.py:76
  160.3 13.8 %reshape.70 = f32[512,4096]{1,0:T(8,128)} reshape(f32[2,1048576]{1,0:T(2,128)} %slice.10) | data formatting | bytes 16777216 | tf_op jit(solution)/shard_map/reshape | solution.py:76
  174.0 47.3 %slice_reduce_fusion = f32[1048576]{0:T(1024)} fusion(f32[3,1048576]{1,0:T(4,128)} %all-gather.3.cloned.1.call-done), kind=kLoop, calls=%fused_computation.12 | loop fusion | bytes 8388608 | tf_op jit(solution)/shard_map/slice | solution.py:77
  221.3 4.9 %reshape.71 = f32[256,4096]{1,0:T(8,128)} reshape(f32[1048576]{0:T(1024)} %slice_reduce_fusion) | data formatting | bytes 8388608 | tf_op jit(solution)/shard_map/reshape | solution.py:77
  226.3 18.1 %select_reduce_fusion.1 = (f32[]{:T(128)}, f32[512,512]{0,1:T(8,128)}) fusion(f32[512,4096]{1,0:T(8,128)} %reshape.70), kind=kOutput, calls=%fused_computation.23 | convolution fusion | flops 12885688320 | bytes 9437188 | tf_op jit(solution)/shard_map/dot_general | solution.py:78
  244.3 9.6 %fusion.20 = f32[512,256]{1,0:T(8,128)S(1)} fusion(f32[512,4096]{1,0:T(8,128)} %reshape.70, f32[256,4096]{1,0:T(8,128)S(1)} %copy-done.4), kind=kOutput, calls=%fused_computation.39 | convolution fusion | flops 6442450944 | bytes 13107200 | tf_op jit(solution)/shard_map/dot_general | solution.py:79
  254.5 2.3 select_reduce_fusion
  256.9 2.6 copy.10
  259.5 1.4 multiply_reduce_fusion.2
  261.5 0.6 multiply_divide_fusion
  262.1 1.2 fusion.12
  263.3 95.0 %while.26 = (s32[]{:T(128)}, f32[512,512]{0,1:T(8,128)}, f32[]{:T(128)}, f32[512,512]{1,0:T(8,128)}, s32[]{:T(128)}) while((s32[]{:T(128)}, f32[512,512]{0,1:T(8,128)}, f32[]{:T(128)}, f32[512,512]{1,0:T(8,128)}, s32[]{:T(128)}) %tuple.48), condition=%wide.region_6.0_spmd.clone, body=%wide.region_4.0_spmd.clone.sunk | while | flops 1612185600 | bytes 12583025 | solution.py:51
  263.3 1.2 copy.37
  264.5 1.0 copy-done.1
  265.5 3.8 multiply_reduce_fusion.5
  270.0 3.9 fusion.62
  273.8 1.2 copy.37
  275.1 1.0 copy-done.1
  276.0 3.8 multiply_reduce_fusion.5
  280.5 3.9 fusion.62
  284.4 1.2 copy.37
  285.6 1.0 copy-done.1
  286.6 3.8 multiply_reduce_fusion.5
  291.1 3.9 fusion.62
  295.0 1.2 copy.37
  296.2 1.0 copy-done.1
  297.2 3.8 multiply_reduce_fusion.5
  301.7 3.9 fusion.62
  305.5 1.2 copy.37
  306.7 1.0 copy-done.1
  307.7 3.8 multiply_reduce_fusion.5
  312.2 3.9 fusion.62
  316.1 1.2 copy.37
  317.3 1.0 copy-done.1
  318.3 3.8 multiply_reduce_fusion.5
  322.8 3.9 fusion.62
  326.6 1.2 copy.37
  327.9 1.0 copy-done.1
  328.8 3.8 multiply_reduce_fusion.5
  333.3 3.9 fusion.62
  337.2 1.2 copy.37
  338.4 1.0 copy-done.1
  339.4 3.8 multiply_reduce_fusion.5
  343.9 3.9 fusion.62
  347.8 1.2 copy.37
  349.0 1.0 copy-done.1
  350.0 3.8 multiply_reduce_fusion.5
  354.5 3.9 fusion.62
  358.3 12.2 %while.27 = (s32[]{:T(128)}, f32[512,512]{0,1:T(8,128)}, f32[]{:T(128)}, f32[512,512]{1,0:T(8,128)}, s32[]{:T(128)}) while((s32[]{:T(128)}, f32[512,512]{0,1:T(8,128)}, f32[]{:T(128)}, f32[512,512]{1,0:T(8,128)}, s32[]{:T(128)}) %tuple.56), condition=%wide.region_9.0_spmd.clone, body=%wide.region_7.0_spmd.clone.sunk | while | flops 3222798336 | bytes 12583025 | solution.py:53
  358.3 1.2 copy.38
  359.5 1.0 copy-done.2
  360.5 4.7 %multiply_reduce_fusion.6 = (f32[]{:T(128)}, f32[512,512]{1,0:T(8,128)}) fusion(f32[512,512]{1,0:T(8,128)} %get-tuple-element.201, f32[512,512]{0,1:T(8,128)S(1)} %copy.38), kind=kOutput, calls=%fused_computation.11.clone.1 | convolution fusion | flops 1611923456 | bytes 3145732 | tf_op jit(solution)/shard_map/while/body/dot_general | solution.py:39
  365.9 4.7 %fusion.67 = f32[512,512]{0,1:T(8,128)} fusion(f32[512,512]{0,1:T(8,128)} %copy-done.2, f32[512,512]{1,0:T(8,128)} %get-tuple-element.171), kind=kOutput, calls=%fused_computation.8.clone.1 | convolution fusion | flops 1610874880 | bytes 3145728 | tf_op jit(solution)/shard_map/while/body/dot_general | solution.py:41
  370.5 3.1 fusion.21
  373.7 3.0 convolution_subtract_fusion.2
  376.7 1.8 fusion.8
  (30 shorter events, 2.1 us)
Async XLA Ops:
  6.5 3.2 copy-start
  6.5 143.8 %all-gather.3.cloned.1.call-start = ((), (), s32[]{:S(2)}) async-start(), calls=%async_computation | async-start | bytes 16842752 | tf_op jit(solution)/shard_map/all_gather | solution.py:74
  12.5 5.2 %copy-start.5 = (bf16[4096,64]{0,1:T(8,128)(2,1)S(1)}, bf16[4096,64]{0,1:T(8,128)(2,1)}, u32[]{:S(2)}) copy-start(bf16[4096,64]{0,1:T(8,128)(2,1)} %param.18) | copy-start | bytes 1572868
  226.3 18.1 %copy-start.4 = (f32[256,4096]{1,0:T(8,128)S(1)}, f32[256,4096]{1,0:T(8,128)}, u32[]{:S(2)}) copy-start(f32[256,4096]{1,0:T(8,128)} %reshape.71) | copy-start | bytes 12582916
  264.5 1.0 copy-start.1
  275.1 1.0 copy-start.1
  285.6 1.0 copy-start.1
  296.2 1.0 copy-start.1
  306.7 1.0 copy-start.1
  317.3 1.0 copy-start.1
  327.9 1.0 copy-start.1
  338.4 1.0 copy-start.1
  349.0 1.0 copy-start.1
  359.5 1.0 copy-start.2
  370.5 6.2 %copy-start.3 = (f32[512,512]{0,1:T(8,128)S(1)}, f32[512,512]{0,1:T(8,128)}, u32[]{:S(2)}) copy-start(f32[512,512]{0,1:T(8,128)} %get-tuple-element.62) | copy-start | bytes 3145732
Sparse Core Ops, SparseCore 0:
  20.9 129.4 all-gather.2
